TPU v7x, 32 devices: a whole 2x2x4 slice. The times are simulated.
32 devices in a mesh: seq: 8 (over z, y), tensor: 2 (over x), section: 2 (over core).
Axes of the slice: x: 2, y: 2, z: 4, core: 2. Of those that a mesh axis runs over, the one named last changes fastest.
Arguments:
- encoder_states: bfloat16 [12288, 4096], P(('seq', 'section'), 'tensor'), may hold values from -6 to 6
- key_weight: bfloat16 [4096, 4096], P(None, 'tensor'), may hold values from -0.125 to 0.125
- value_weight: bfloat16 [4096, 4096], P(None, 'tensor'), may hold values from -0.125 to 0.125
- queries: bfloat16 [4096, 4096], P(('seq', 'section'), 'tensor'), may hold values from -400 to 400
- out_grad: bfloat16 [4096, 4096], P(('seq', 'section'), 'tensor'), may hold values from -6 to 6
- band_blocks: int32 [32, 2], P(('seq', 'section')), may hold values from 0 to 95, as said below
Outputs:
- query_grad: bfloat16 [4096, 4096], P(('seq', 'section'), 'tensor')
- encoder_grad: bfloat16 [12288, 4096], P(('seq', 'section'), 'tensor')
Inputs may be any that keep to these rules, and one draw needn't show every extreme that they name: band_blocks[b] holds the first and the last encoder block (inclusive, blocks of 128 frames) that decoder block b attends to; both rise with b; the first lies in 3 * b - 2 to 3 * b - 1 and the last in 3 * b + 3 to 3 * b + 4, each clipped to the encoder's blocks; some band spans exactly 7 encoder blocks.
All inputs are finite; a program needn't handle non-finite values.
Results may differ from a plain program's by a relative error of at most 0.006.
The roundings to bfloat16 on the way count: a program that leaves them out, or rounds other values in their place, can miss the bound.
Values may be sent and summed in bfloat16 or wider, within the bound.
No kernel may reach another device: no remote copies, remote signals or barrier semaphores. Data moves between devices by JAX's collectives and lax.ppermute only.
A program may use at most 192 MiB of HBM per device.

v0:
```python
import jax
import jax.numpy as jnp
from jax import lax
from jax.sharding import PartitionSpec as P

DH = 128
BLOCK = 128
HALO_BLK = 2


def with_halo(shard, sides, width):
    for axis, dim in sides:
        size, length = (lax.axis_size(axis), shard.shape[dim])
        up = [(i, (i + 1) % size) for i in range(size - 1)]
        down = [(j, i) for i, j in up]
        last = lax.slice_in_dim(shard, length - width, length, axis=dim)
        first = lax.slice_in_dim(shard, 0, width, axis=dim)
        before = lax.ppermute(last, axis, up)
        after = lax.ppermute(first, axis, down)
        shard = jnp.concatenate([before, shard, after], axis=dim)
    return shard


def shifted(value, axis, steps):
    count = lax.axis_size(axis)
    first, last = (max(0, -steps), min(count, count - steps))
    return lax.ppermute(value, axis, [(source, source + steps) for source in range(first, last)])


def attend(query_rows, grad_rows, key_rows, value_rows, allowed, softmax_scale):
    scores = (
        jnp.einsum("qhd,khd->hqk", query_rows, key_rows, preferred_element_type=jnp.float32)
        * softmax_scale
    )
    row_max = jnp.max(jnp.where(allowed[None], scores, -jnp.inf), axis=-1, keepdims=True)
    unnormed = jnp.where(
        allowed[None], jnp.exp(jnp.where(allowed[None], scores, row_max) - row_max), 0.0
    )
    probability = unnormed / jnp.sum(unnormed, axis=-1, keepdims=True)
    probability_low = probability.astype(jnp.bfloat16)
    attended = jnp.einsum(
        "hqk,khd->qhd", probability_low, value_rows, preferred_element_type=jnp.float32
    )
    row_delta = jnp.sum(grad_rows.astype(jnp.float32) * attended, axis=-1)
    prob_grad = jnp.einsum(
        "qhd,khd->hqk", grad_rows, value_rows, preferred_element_type=jnp.float32
    )
    score_grad = (
        probability * (prob_grad - jnp.transpose(row_delta)[:, :, None]) * softmax_scale
    ).astype(jnp.bfloat16)
    query_grad = jnp.einsum(
        "hqk,khd->qhd", score_grad, key_rows, preferred_element_type=jnp.float32
    ).astype(jnp.bfloat16)
    key_part = jnp.einsum(
        "hqk,qhd->khd", score_grad, query_rows, preferred_element_type=jnp.float32
    )
    value_part = jnp.einsum(
        "hqk,qhd->khd", probability_low, grad_rows, preferred_element_type=jnp.float32
    )
    return (query_grad, key_part, value_part)


def on_device(encoder_states, key_weight, value_weight, queries, out_grad, band_blocks):
    frames = encoder_states.shape[0]
    tokens = queries.shape[0]
    columns = key_weight.shape[1]
    head_count = columns // DH
    softmax_scale = DH ** (-0.5)
    margin = HALO_BLK * BLOCK
    extent = frames + 2 * margin
    contract = (((1,), (1,)), ((), ()))
    pieces_in = lax.all_gather(encoder_states, "tensor", axis=1, tiled=True)
    keys_wide = jnp.dot(pieces_in, key_weight, preferred_element_type=jnp.float32)
    values_wide = jnp.dot(pieces_in, value_weight, preferred_element_type=jnp.float32)
    stacked = jnp.concatenate(
        [keys_wide.astype(jnp.bfloat16), values_wide.astype(jnp.bfloat16)], axis=1
    )
    extended = with_halo(stacked, ((("seq", "section"), 0),), margin)
    ext_keys = extended[:, :columns].reshape(extent, head_count, DH)
    ext_values = extended[:, columns:].reshape(extent, head_count, DH)
    anchor = lax.axis_index(("seq", "section")) * frames - margin
    lower_edge = band_blocks[:, 0] * BLOCK - anchor
    upper_edge = (band_blocks[:, 1] + 1) * BLOCK - anchor
    query_all = queries.reshape(tokens, head_count, DH)
    grad_all = out_grad.reshape(tokens, head_count, DH)
    lower_row = jnp.repeat(lower_edge, BLOCK)
    upper_row = jnp.repeat(upper_edge, BLOCK)
    position = jnp.arange(extent, dtype=jnp.int32)
    allowed = (position[None, :] >= lower_row[:, None]) & (position[None, :] < upper_row[:, None])
    row_qgrad, key_part, value_part = attend(
        query_all, grad_all, ext_keys, ext_values, allowed, softmax_scale
    )
    grads = jnp.concatenate(
        [key_part.reshape(extent, columns), value_part.reshape(extent, columns)], axis=1
    )
    query_grad = row_qgrad.reshape(tokens, columns)
    from_below = shifted(grads[extent - margin :], ("seq", "section"), 1)
    from_above = shifted(grads[:margin], ("seq", "section"), -1)
    own_rows = grads[margin : margin + frames]
    own_rows = jnp.concatenate(
        [
            own_rows[:margin] + from_below,
            own_rows[margin : frames - margin],
            own_rows[frames - margin :] + from_above,
        ],
        axis=0,
    )
    kv_grad = own_rows.astype(jnp.bfloat16)
    key_grad = kv_grad[:, :columns]
    value_grad = kv_grad[:, columns:]
    group_term = lax.dot_general(key_grad, key_weight, contract, preferred_element_type=jnp.float32)
    group_term = group_term + lax.dot_general(
        value_grad, value_weight, contract, preferred_element_type=jnp.float32
    )
    encoder_grad = lax.psum_scatter(
        group_term.astype(jnp.bfloat16), "tensor", scatter_dimension=1, tiled=True
    )
    return (query_grad, encoder_grad)


def solution(mesh):
    return jax.shard_map(
        on_device,
        mesh=mesh,
        in_specs=(
            P(("seq", "section"), "tensor"),
            P(None, "tensor"),
            P(None, "tensor"),
            P(("seq", "section"), "tensor"),
            P(("seq", "section"), "tensor"),
            P(("seq", "section"), None),
        ),
        out_specs=(P(("seq", "section"), "tensor"), P(("seq", "section"), "tensor")),
        check_vma=False,
    )
```

profile of v0, /device:TPU:0, one launch (start us, length us, event | category | flops | bytes accessed | tf_op | source)
XLA Modules:
  0.0 583.7 jit_solution(2471942912574353131)
XLA Ops:
  7.2 0.0 all-gather.2.cloned.1.call-start
  7.2 0.7 all-gather.2.cloned.1.call-update
  7.9 0.0 reduce-scatter.2.cloned.1.call-start
  7.9 84.7 %all-gather.2.cloned.1.call-done = bf16[768,4096]{1,0:T(8,128)(2,1)} async-done(((bf16[768,2048]{1,0:T(8,128)(2,1)}), bf16[768,4096]{1,0:T(8,128)(2,1)}) %all-gather.2.cloned.1.call-update) | async-done | bytes 6291472 | tf_op jit(solution)/shard_map/all_gather | solution.py:72
  92.6 0.0 copy-start.5
  92.6 20.6 %convolution_convert_fusion = bf16[768,2048]{1,0:T(8,128)(2,1)S(1)} fusion(bf16[768,4096]{1,0:T(8,128)(2,1)} %all-gather.2.cloned.1.call-done, bf16[4096,2048]{1,0:T(8,128)(2,1)} %param.8), kind=kOutput, calls=%fused_computation.37 | convolution fusion | flops 12886474752 | bytes 26214400 | tf_op jit(solution)/shard_map/dot_general | solution.py:74
  113.2 0.0 copy-done.5
  113.2 16.8 %convolution_convert_fusion.1 = bf16[768,2048]{1,0:T(8,128)(2,1)S(1)} fusion(bf16[768,4096]{1,0:T(8,128)(2,1)S(1)} %copy-done.5, bf16[4096,2048]{1,0:T(8,128)(2,1)} %param.7), kind=kOutput, calls=%fused_computation.38 | convolution fusion | flops 12886474752 | bytes 26214400 | tf_op jit(solution)/shard_map/dot_general | solution.py:73
  130.1 0.0 copy-start.1
  130.1 1.7 copy-done.1
  131.8 0.0 copy-start.4
  131.8 2.3 pad_maximum_fusion.4
  134.1 1.3 collective-permute-start.1
  135.4 4.6 collective-permute-start
  140.0 2.3 copy.10
  142.2 2.3 copy.27
  144.5 0.0 copy-done.4
  144.5 0.2 subtract_reduce_fusion.1
  144.7 0.1 broadcast_bitcast_fusion
  144.7 0.3 fusion.27
  145.1 0.0 collective-permute-done.1
  145.1 0.0 collective-permute-done
  145.1 18.8 %pad_maximum_fusion = bf16[1280,4096]{1,0:T(8,128)(2,1)} fusion(bf16[256,4096]{1,0:T(8,128)(2,1)} %collective-permute-done.1, bf16[768,2048]{1,0:T(8,128)(2,1)S(1)} %convolution_convert_fusion, bf16[768,2048]{1,0:T(8,128)(2,1)} %copy-done.1, bf16[256,4096]{1,0:T(8,128)(2,1)} %collective-permute-done), kind=kLoop, calls=%fused_computation.21 | loop fusion | flops 41943040 | bytes 20971520 | tf_op jit(solution)/shard_map/concatenate | solution.py:20
  163.9 10.1 %fusion.30 = (bf16[1280,2048]{1,0:T(8,128)(2,1)}, bf16[1280,2048]{1,0:T(8,128)(2,1)}) fusion(bf16[1280,4096]{1,0:T(8,128)(2,1)} %pad_maximum_fusion), kind=kLoop, calls=%fused_computation.54 | loop fusion | bytes 20971520 | tf_op jit(solution)/shard_map/slice | solution.py:80
  174.0 0.0 copy-start.2
  174.0 7.9 %copy.26 = bf16[1280,2048]{0,1:T(8,128)(2,1)} copy(bf16[1280,2048]{1,0:T(8,128)(2,1)} %get-tuple-element.9) | data formatting | bytes 10485760 | tf_op jit(solution)/shard_map/reshape | solution.py:79
  181.9 7.8 %copy.28 = bf16[1280,2048]{0,1:T(8,128)(2,1)} copy(bf16[1280,2048]{1,0:T(8,128)(2,1)} %get-tuple-element.8) | data formatting | bytes 10485760 | tf_op jit(solution)/shard_map/reshape | solution.py:80
  189.7 0.0 copy-done.2
  189.7 13.1 %fusion.2 = (f32[16,256]{1,0:T(8,128)S(1)}, f32[16,1280,256]{2,1,0:T(8,128)}) fusion(pred[256,1280]{0,1:T(8,128)(4,1)S(1)} %fusion.27, bf16[1280,16,128]{0,2,1:T(8,128)(2,1)} %bitcast.77, bf16[256,16,128]{0,2,1:T(8,128)(2,1)S(1)} %bitcast.79), kind=kOutput, calls=%fused_computation.13 | convolution fusion | flops 1357901824 | bytes 27607040 | tf_op jit(solution)/shard_map/qhd,khd->hqk/dot_general | solution.py:32
  202.8 0.0 copy-start.3
  202.8 0.0 slice-start.3
  202.8 10.3 %fusion.7 = f32[16,256]{1,0:T(8,128)S(1)} fusion(f32[16,1280,256]{2,1,0:T(8,128)} %get-tuple-element.13, f32[16,256]{1,0:T(8,128)S(1)} %get-tuple-element.12, pred[256,1280]{0,1:T(8,128)(4,1)S(1)} %fusion.27), kind=kLoop, calls=%fused_computation.19 | loop fusion | flops 20967424 | bytes 21331968 | tf_op jit(solution)/shard_map/reduce_sum | solution.py:39
  213.1 0.0 copy-done.3
  213.1 0.0 slice-start.4
  213.1 13.1 %fusion.8 = f32[16,1280,128]{1,2,0:T(8,128)} fusion(bf16[256,16,128]{0,2,1:T(8,128)(2,1)S(1)} %bitcast.86, f32[16,1280,256]{2,1,0:T(8,128)} %get-tuple-element.13, f32[16,256]{1,0:T(8,128)S(1)} %fusion.7, f32[16,256]{1,0:T(8,128)S(1)} %get-tuple-element.12, pred[256,1280]{0,1:T(8,128)(4,1)S(1)} %fusion.27), kind=kOutput, calls=%fused_computation.23 | convolution fusion | flops 1368391680 | bytes 32866304 | tf_op jit(solution)/shard_map/hqk,qhd->khd/dot_general | solution.py:57
  226.2 0.0 slice-done.3
  226.2 0.0 slice-done.4
  226.2 10.5 %fusion.24 = f32[256,16]{0,1:T(8,128)S(1)} fusion(bf16[256,16,128]{0,2,1:T(8,128)(2,1)S(1)} %bitcast.87, bf16[1280,16,128]{0,2,1:T(8,128)(2,1)S(1)} %bitcast.85, f32[16,1280,256]{2,1,0:T(8,128)} %get-tuple-element.13, f32[16,256]{1,0:T(8,128)S(1)} %fusion.7, f32[16,256]{1,0:T(8,128)S(1)} %get-tuple-element.12, pred[256,1280]{0,1:T(8,128)(4,1)S(1)} %fusion.27), kind=kOutput, calls=%fused_computation.45 | convolution fusion | flops 1369960448 | bytes 27639808 | tf_op jit(solution)/shard_map/hqk,khd->qhd/dot_general | solution.py:41
  236.7 15.2 %fusion.1 = bf16[16,256,1280]{1,2,0:T(8,128)(2,1)} fusion(bf16[1280,16,128]{0,2,1:T(8,128)(2,1)} %bitcast.82, bf16[256,16,128]{0,2,1:T(8,128)(2,1)S(1)} %bitcast.88, f32[16,256]{1,0:T(8,128)S(1)} %bitcast.89, f32[16,256]{1,0:T(8,128)S(1)} %fusion.7, f32[16,256]{1,0:T(8,128)S(1)} %get-tuple-element.12, f32[16,1280,256]{2,1,0:T(8,128)} %get-tuple-element.13, ...), kind=kOutput, calls=%fused_computation.10 | convolution fusion | flops 1384120320 | bytes 38125568 | tf_op jit(solution)/shard_map/qhd,khd->hqk/dot_general | solution.py:45
  251.9 11.5 %fusion.31 = f32[16,1280,128]{1,2,0:T(8,128)} fusion(bf16[16,256,1280]{1,2,0:T(8,128)(2,1)} %fusion.1, bf16[256,16,128]{0,2,1:T(8,128)(2,1)S(1)} %bitcast.80), kind=kOutput, calls=%fused_computation.55 | convolution fusion | flops 1342177280 | bytes 22020096 | tf_op jit(solution)/shard_map/hqk,qhd->khd/dot_general | solution.py:54
  263.4 0.0 copy-start
  263.4 0.0 slice-start
  263.4 0.0 slice-start.1
  263.4 2.7 fusion.18
  266.1 0.0 slice-start.2
  266.1 41.4 %collective-permute-start.2 = (f32[256,4096]{0,1:T(8,128)S(1)}, f32[256,4096]{0,1:T(8,128)S(1)}, u32[]{:S(2)}, u32[]{:S(2)}) collective-permute-start(f32[256,4096]{0,1:T(8,128)S(1)} %fusion.18), channel_id=1, source_target_pairs={{0,1},{1,4},{4,5},{5,8},{8,9},{9,12},{12,13},{13,16},{16,17},{17,2... | collective-permute-start | bytes 12582920 | tf_op jit(solution)/shard_map/ppermute | solution.py:27
  307.5 6.5 %collective-permute-done.2 = f32[256,4096]{0,1:T(8,128)S(1)} collective-permute-done((f32[256,4096]{0,1:T(8,128)S(1)}, f32[256,4096]{0,1:T(8,128)S(1)}, u32[]{:S(2)}, u32[]{:S(2)}) %collective-permute-start.2) | collective-permute-done | bytes 4194336 | tf_op jit(solution)/shard_map/ppermute | solution.py:27
  314.0 0.0 copy-done
  314.0 3.0 fusion.17
  316.9 1.3 collective-permute-start.3
  318.2 0.0 slice-done
  318.3 0.0 slice-done.1
  318.3 0.0 slice-done.2
  318.3 0.2 fusion.20
  318.5 93.4 %collective-permute-done.3 = f32[256,4096]{0,1:T(8,128)} collective-permute-done((f32[256,4096]{0,1:T(8,128)S(1)}, f32[256,4096]{0,1:T(8,128)}, u32[]{:S(2)}, u32[]{:S(2)}) %collective-permute-start.3) | collective-permute-done | bytes 4194336 | tf_op jit(solution)/shard_map/ppermute | solution.py:27
  411.9 2.6 fusion.14
  414.5 3.2 pad_maximum_fusion.1
  417.7 20.3 %fusion.22 = f32[768,4096]{1,0:T(8,128)} fusion(bf16[4096,2048]{1,0:T(8,128)(2,1)} %param.7, bf16[768,4096]{0,1:T(8,128)(2,1)} %pad_maximum_fusion.1), kind=kOutput, calls=%fused_computation.40 | convolution fusion | flops 12884901888 | bytes 32505856 | tf_op jit(solution)/shard_map/dot_general | solution.py:111
  438.0 21.6 %add_convert_fusion = bf16[768,4096]{1,0:T(8,128)(2,1)} fusion(f32[768,4096]{1,0:T(8,128)} %fusion.22, bf16[4096,2048]{1,0:T(8,128)(2,1)} %param.8, bf16[768,4096]{0,1:T(8,128)(2,1)} %pad_maximum_fusion.1), kind=kOutput, calls=%fused_computation.20 | convolution fusion | flops 12891193344 | bytes 38797312 | tf_op jit(solution)/shard_map/dot_general | solution.py:112
  459.5 0.0 reduce-scatter.2.cloned.1.call-update
  459.6 7.1 %convolution_convert_fusion.2 = bf16[16,128,256]{2,1,0:T(8,128)(2,1)S(1)} fusion(bf16[1280,16,128]{0,2,1:T(8,128)(2,1)} %bitcast.78, bf16[16,256,1280]{1,2,0:T(8,128)(2,1)} %fusion.1), kind=kOutput, calls=%fused_computation.46 | convolution fusion | flops 1342701568 | bytes 16777216 | tf_op jit(solution)/shard_map/hqk,khd->qhd/dot_general | solution.py:51
  466.7 1.4 copy.20
  468.1 108.6 %reduce-scatter.2.cloned.1.call-done = bf16[768,2048]{1,0:T(8,128)(2,1)} async-done(((bf16[768,4096]{1,0:T(8,128)(2,1)}), bf16[768,2048]{1,0:T(8,128)(2,1)}) %reduce-scatter.2.cloned.1.call-update) | async-done | bytes 3145744 | tf_op jit(solution)/shard_map/reduce_scatter | solution.py:115
  (2 shorter events, 0.0 us)
Async XLA Ops:
  7.2 85.5 %all-gather.2.cloned.1.call-start = ((), (), s32[]{:S(2)}) async-start(), calls=%async_computation.1 | async-start | bytes 9437184 | tf_op jit(solution)/shard_map/all_gather | solution.py:72
  7.9 568.8 %reduce-scatter.2.cloned.1.call-start = ((), (), s32[]{:S(2)}) async-start(), calls=%async_computation.2 | async-start | bytes 9437184 | tf_op jit(solution)/shard_map/reduce_scatter | solution.py:115
  92.6 20.6 %copy-start.5 = (bf16[768,4096]{1,0:T(8,128)(2,1)S(1)}, bf16[768,4096]{1,0:T(8,128)(2,1)}, u32[]{:S(2)}) copy-start(bf16[768,4096]{1,0:T(8,128)(2,1)} %all-gather.2.cloned.1.call-done) | copy-start | bytes 18874372
  130.1 1.7 copy-start.1
  131.8 12.7 %copy-start.4 = (s32[2,2]{1,0:T(2,128)S(1)}, s32[2,2]{1,0:T(2,128)}, u32[]{:S(2)}) copy-start(s32[2,2]{1,0:T(2,128)} %param.11) | copy-start | bytes 52
  134.1 11.0 %collective-permute-start.1 = (bf16[256,4096]{1,0:T(8,128)(2,1)}, bf16[256,4096]{1,0:T(8,128)(2,1)}, u32[]{:S(2)}, u32[]{:S(2)}) collective-permute-start(bf16[256,4096]{1,0:T(8,128)(2,1)} %get-tuple-element.11), channel_id=1, source_target_pairs={{1,0},{4,1},{5,4},{8,5},{9,8},{12,9},{13,12},{16,13},{17,16},{20,1... | collective-permute-start | bytes 6291464 | tf_op jit(solution)/shard_map/ppermute | solution.py:19
  135.4 9.7 %collective-permute-start = (bf16[256,4096]{1,0:T(8,128)(2,1)}, bf16[256,4096]{1,0:T(8,128)(2,1)}, u32[]{:S(2)}, u32[]{:S(2)}) collective-permute-start(bf16[256,4096]{1,0:T(8,128)(2,1)} %get-tuple-element.10), channel_id=1, source_target_pairs={{0,1},{1,4},{4,5},{5,8},{8,9},{9,12},{12,13},{13,16},{16,17},{17,2... | collective-permute-start | bytes 6291464 | tf_op jit(solution)/shard_map/ppermute | solution.py:18
  174.0 15.7 %copy-start.2 = (bf16[256,2048]{0,1:T(8,128)(2,1)S(1)}, bf16[256,2048]{0,1:T(8,128)(2,1)}, u32[]{:S(2)}) copy-start(bf16[256,2048]{0,1:T(8,128)(2,1)} %copy.27) | copy-start | bytes 3145732
  202.8 10.3 %copy-start.3 = (bf16[256,2048]{0,1:T(8,128)(2,1)S(1)}, bf16[256,2048]{0,1:T(8,128)(2,1)}, u32[]{:S(2)}) copy-start(bf16[256,2048]{0,1:T(8,128)(2,1)} %copy.10) | copy-start | bytes 3145732
  202.8 23.4 %slice-start.3 = ((s8[5242880]{0:T(1024)(128)(4,1)}), s8[4194304]{0:T(1024)(128)(4,1)S(1)}, s32[]{:S(2)}) async-start(s8[5242880]{0:T(1024)(128)(4,1)} %bitcast.83), calls=%async_computation.6 | async-start | bytes 8388608
  213.1 13.1 %slice-start.4 = ((s8[5242880]{0:T(1024)(128)(4,1)}), s8[1048576]{0:T(1024)(128)(4,1)S(1)}, s32[]{:S(2)}) async-start(s8[5242880]{0:T(1024)(128)(4,1)} %bitcast.83), calls=%async_computation.7 | async-start | bytes 2097152
  263.4 50.6 %copy-start = (f32[16,1280,128]{1,2,0:T(8,128)S(1)}, f32[16,1280,128]{1,2,0:T(8,128)}, u32[]{:S(2)}) copy-start(f32[16,1280,128]{1,2,0:T(8,128)} %fusion.31) | copy-start | bytes 31457284
  263.4 54.9 %slice-start = ((s8[10485760]{0:T(1024)(128)(4,1)}), s8[4194304]{0:T(1024)(128)(4,1)S(1)}, s32[]{:S(2)}) async-start(s8[10485760]{0:T(1024)(128)(4,1)} %bitcast.73), calls=%async_computation.3 | async-start | bytes 8388608
  263.4 54.9 %slice-start.1 = ((s8[10485760]{0:T(1024)(128)(4,1)}), s8[4194304]{0:T(1024)(128)(4,1)S(1)}, s32[]{:S(2)}) async-start(s8[10485760]{0:T(1024)(128)(4,1)} %bitcast.73), calls=%async_computation.4 | async-start | bytes 8388608
  266.1 52.2 %slice-start.2 = ((s8[10485760]{0:T(1024)(128)(4,1)}), s8[2097152]{0:T(1024)(128)(4,1)S(1)}, s32[]{:S(2)}) async-start(s8[10485760]{0:T(1024)(128)(4,1)} %bitcast.73), calls=%async_computation.5 | async-start | bytes 4194304
  266.1 47.9 %collective-permute-start.2 = (f32[256,4096]{0,1:T(8,128)S(1)}, f32[256,4096]{0,1:T(8,128)S(1)}, u32[]{:S(2)}, u32[]{:S(2)}) collective-permute-start(f32[256,4096]{0,1:T(8,128)S(1)} %fusion.18), channel_id=1, source_target_pairs={{0,1},{1,4},{4,5},{5,8},{8,9},{9,12},{12,13},{13,16},{16,17},{17,2... | collective-permute-start | bytes 12582920 | tf_op jit(solution)/shard_map/ppermute | solution.py:27
  316.9 94.9 %collective-permute-start.3 = (f32[256,4096]{0,1:T(8,128)S(1)}, f32[256,4096]{0,1:T(8,128)}, u32[]{:S(2)}, u32[]{:S(2)}) collective-permute-start(f32[256,4096]{0,1:T(8,128)S(1)} %get-tuple-element.7), channel_id=1, source_target_pairs={{1,0},{4,1},{5,4},{8,5},{9,8},{12,9},{13,12},{16,13},{17,16},{20,1... | collective-permute-start | bytes 12582920 | tf_op jit(solution)/shard_map/ppermute | solution.py:27
Sparse Core Ops, SparseCore 0:
  9.5 83.0 all-gather.1
  459.7 116.9 reduce-scatter.1
where the time goes:
time: 592 us; the launch traced here: 584 us
  waiting for transfers between devices  294 us (50%)
  matrix products  150 us (25%)
  starting transfers between devices  48.6 us (8%)
  other arithmetic  43.5 us (7%)
  local copies, waits for them, and re-layouts  33.6 us (6%)
  between operations  14.4 us (2%)
    reduce_scatter x1, waiting for transfers between devices, on_device(): lax.psum_scatter(group_term.astype(jnp.bfloat16), 'tensor', scatter_dimen...  109 us
    ppermute x2, waiting for transfers between devices, shifted(): lax.ppermute(value, axis, [(source, source + steps) for source in range(f...  99.9 us
    all_gather x1, waiting for transfers between devices, on_device(): pieces_in = lax.all_gather(encoder_states, 'tensor', axis=1, tiled=True)  84.7 us
    ppermute x2, starting transfers between devices, shifted(): lax.ppermute(value, axis, [(source, source + steps) for source in range(f...  42.7 us
    dot_general x1, matrix products, on_device(): lax.dot_general(value_grad, value_weight, contract, preferred_element_typ...  21.6 us
    dot_general x1, matrix products, on_device(): jnp.dot(pieces_in, value_weight, preferred_element_type=jnp.float32)  20.6 us
    dot_general x1, matrix products, on_device(): lax.dot_general(key_grad, key_weight, contract, preferred_element_type=jn...  20.3 us
    concatenate x1, other arithmetic, with_halo(): shard = jnp.concatenate([before, shard, after], axis=dim)  18.8 us
  transfers between devices with their start and end apart: 6, of which 4 were waited for; matrix products, arithmetic and copies ran while one was open for 2% of the time, Pallas kernels for 0%

commit v1 on v0

v1 whole, which is shorter than its diff:
```python
import functools

import jax
import jax.numpy as jnp
from jax import lax
from jax.experimental import pallas as pl
from jax.experimental.pallas import tpu as pltpu
from jax.sharding import PartitionSpec as P

DH = 128
BLOCK = 128
RATIO = 3
HALO_BLK = 2
NEG = -1e30
ROWS = ("seq", "section")
NT = (((1,), (1,)), ((), ()))
TN = (((0,), (0,)), ((), ()))
F32 = jnp.float32
BF16 = jnp.bfloat16


def call(body, grid, scalars, in_specs, out_specs, out_shape, flops, moved, aliases=None, name=None):
    return pl.pallas_call(
        body,
        grid_spec=pltpu.PrefetchScalarGridSpec(
            num_scalar_prefetch=scalars, grid=grid, in_specs=in_specs, out_specs=out_specs
        ),
        out_shape=out_shape,
        input_output_aliases=aliases or {},
        cost_estimate=pl.CostEstimate(flops=flops, bytes_accessed=moved, transcendentals=0),
        name=name,
    )


def project_own(index, states, key_weight, value_weight, cuts):
    rows, depth = states.shape
    columns = key_weight.shape[1]
    wide = min(256, columns)

    def body(index_ref, states_ref, key_ref, value_ref, *outs):
        for at, weight_ref in enumerate((key_ref, value_ref)):
            product = jnp.dot(states_ref[...], weight_ref[...], preferred_element_type=F32)
            for piece, (first, last) in enumerate(cuts):
                outs[2 * piece + at][...] = product[first:last]

    weight_spec = pl.BlockSpec((depth, wide), lambda j, index_ref: (index_ref[0], j))
    shapes, specs = [], []
    for first, last in cuts:
        for _ in range(2):
            shapes.append(jax.ShapeDtypeStruct((last - first, columns), F32))
            specs.append(pl.BlockSpec((last - first, wide), lambda j, index_ref: (0, j)))
    out = call(
        body,
        (columns // wide,),
        1,
        [pl.BlockSpec((rows, depth), lambda j, index_ref: (0, 0)), weight_spec, weight_spec],
        specs,
        shapes,
        4 * rows * depth * columns,
        2 * rows * depth + 4 * depth * columns + 8 * rows * columns,
        name="project_own",
    )(index, states, key_weight, value_weight)
    return [(out[2 * i], out[2 * i + 1]) for i in range(len(cuts))]


def project_rest(index, partial, arrived, key_weight, value_weight):
    rows, columns = partial[0].shape
    depth = arrived[0].shape[1]
    count = len(arrived)
    wide = min(256, columns)

    def body(index_ref, *refs):
        key_part, value_part = refs[:2]
        pieces = refs[2 : 2 + count]
        weights = (refs[2 + count : 2 + 2 * count], refs[2 + 2 * count : 2 + 3 * count])
        outs = refs[2 + 3 * count :]
        for part_ref, weight_refs, out_ref in zip((key_part, value_part), weights, outs):
            total = part_ref[...]
            for piece_ref, weight_ref in zip(pieces, weight_refs):
                total = total + jnp.dot(piece_ref[...], weight_ref[...], preferred_element_type=F32)
            out_ref[...] = total.astype(BF16)

    tile = pl.BlockSpec((rows, wide), lambda j, index_ref: (0, j))
    piece_spec = pl.BlockSpec((rows, depth), lambda j, index_ref: (0, 0))
    weight_specs = [
        pl.BlockSpec((depth, wide), lambda j, index_ref, k=k: (index_ref[k + 1], j))
        for k in range(count)
    ]
    return call(
        body,
        (columns // wide,),
        1,
        [tile, tile] + [piece_spec] * count + weight_specs * 2,
        [tile, tile],
        [jax.ShapeDtypeStruct((rows, columns), BF16)] * 2,
        4 * rows * depth * columns * count,
        count * (2 * rows * depth + 4 * depth * columns) + 12 * rows * columns,
        name="project_rest",
    )(index, *partial, *arrived, *([key_weight] * count), *([value_weight] * count))


def certain(token, frame):
    return RATIO * token - 1 <= frame <= RATIO * token + RATIO


def reaches(token, frame):
    return RATIO * token - HALO_BLK <= frame <= RATIO * token + RATIO - 1 + HALO_BLK


class Tiles:
    def __init__(self, tokens, first, last, halo):
        self.first, self.last, self.tokens = first, last, tokens
        low, high = (-1, tokens + 1) if halo else (0, tokens)
        touched = [
            t for t in range(low, high) if any(reaches(t, f) for f in range(first, last))
        ]
        whole = [t for t in touched if all(reaches(t, f) for f in range(first, last))]
        self.groups = []
        if whole:
            self.groups.append((whole, first, last))
        for t in touched:
            if t not in whole:
                frames = [f for f in range(first, last) if reaches(t, f)]
                self.groups.append(([t], frames[0], frames[-1] + 1))
        self.touched = touched


def token_rows(refs, tokens, own_count, lanes):
    below, own, above = refs
    pieces = []
    for t in tokens:
        if t < 0:
            pieces.append(below[:, lanes])
        elif t >= own_count:
            pieces.append(above[:, lanes])
        else:
            pieces.append(own[t * BLOCK : (t + 1) * BLOCK, lanes])
    return pieces[0] if len(pieces) == 1 else jnp.concatenate(pieces, axis=0)


def tile_allowed(band_ref, token, frame, own_count):
    if 0 <= token < own_count and certain(token, frame):
        return None
    return (band_ref[2 * (token + 1)] <= frame) & (frame <= band_ref[2 * (token + 1) + 1])


def head_tiles(band_ref, tiles, own_count, key_ref, value_ref, query_refs, grad_refs, lanes, scale):
    for tokens, first, last in tiles.groups:
        rows = slice((first - tiles.first) * BLOCK, (last - tiles.first) * BLOCK)
        keys, values = key_ref[rows, lanes], value_ref[rows, lanes]
        query_rows = token_rows(query_refs, tokens, own_count, lanes)
        grad_rows = token_rows(grad_refs, tokens, own_count, lanes)
        scores = lax.dot_general(keys, query_rows, NT, preferred_element_type=F32) * scale
        slopes = lax.dot_general(values, grad_rows, NT, preferred_element_type=F32)
        yield tokens, first, last, keys, query_rows, grad_rows, scores, slopes


def piece(array, frame, position):
    return array[frame * BLOCK : (frame + 1) * BLOCK, position * BLOCK : (position + 1) * BLOCK]


def fold(stats):
    tops = [jnp.where(total > 0, top, NEG) for top, total, _ in stats]
    top = functools.reduce(jnp.maximum, tops)
    gains = [jnp.exp(t - top) for t in tops]
    total = sum(g * s[1] for g, s in zip(gains, stats))
    weighted = sum(g * s[2] for g, s in zip(gains, stats))
    return top, total, weighted


def tile_stats(band_ref, tiles_list, own_count, kv_refs, query_refs, grad_refs, lanes, scale):
    found = {}
    for tiles, (key_ref, value_ref) in zip(tiles_list, kv_refs):
        for tokens, first, last, _, _, _, scores, slopes in head_tiles(
            band_ref, tiles, own_count, key_ref, value_ref, query_refs, grad_refs, lanes, scale
        ):
            for position, t in enumerate(tokens):
                for f in range(first, last):
                    allowed = tile_allowed(band_ref, t, f, own_count)
                    found.setdefault(t, []).append(
                        (allowed, piece(scores, f - first, position), piece(slopes, f - first, position))
                    )
    stats = {}
    for t, entries in found.items():
        shown = [s if a is None else jnp.where(a, s, NEG) for a, s, _ in entries]
        top = jnp.max(functools.reduce(jnp.maximum, shown), axis=0, keepdims=True)
        total = weighted = None
        for (allowed, _, slope), s in zip(entries, shown):
            e = jnp.exp(s - top)
            if allowed is not None:
                e = jnp.where(allowed, e, 0.0)
            total = e if total is None else total + e
            weighted = e * slope if weighted is None else weighted + e * slope
        stats[t] = (
            top,
            jnp.sum(total, axis=0, keepdims=True),
            jnp.sum(weighted, axis=0, keepdims=True),
        )
    return stats


def read_stats(ref, head, row):
    return tuple(ref[head, row + i : row + i + 1, :] for i in range(3))


def write_stats(ref, head, row, stats):
    for i, value in enumerate(stats):
        ref[head, row + i : row + i + 1, :] = value


def token_specs(own_count, wide, head_blocks):
    halo_q = pl.BlockSpec((BLOCK, wide), lambda h, band_ref: (0, h))
    halo_g = pl.BlockSpec((BLOCK, wide), lambda h, band_ref: (0, h + head_blocks))
    own = pl.BlockSpec((own_count * BLOCK, wide), lambda h, band_ref: (0, h))
    return [halo_q, own, halo_q, halo_g, own, halo_g]


def row_stats(band, tiles_list, kvs, queries, grads, below, above, earlier, scale):
    own_count = queries.shape[0] // BLOCK
    columns = queries.shape[1]
    heads = columns // DH
    per = min(2, heads)
    wide = per * DH
    depth = -(-3 * (own_count + 2) // 8) * 8
    count = len(kvs)

    def body(band_ref, *refs):
        tokens = refs[:6]
        kv_refs = [refs[6 + 2 * i : 8 + 2 * i] for i in range(count)]
        rest = refs[6 + 2 * count :]
        out_ref = rest[-1]
        for head in range(per):
            lanes = slice(head * DH, (head + 1) * DH)
            stats = tile_stats(
                band_ref, tiles_list, own_count, kv_refs, tokens[:3], tokens[3:], lanes, scale
            )
            for t in range(-1, own_count + 1):
                row = 3 * (t + 1)
                mine = [stats[t]] if t in stats else []
                if earlier is not None:
                    mine.append(read_stats(rest[0], head, row))
                if len(mine) == 2:
                    mine = [fold(mine)]
                write_stats(out_ref, head, row, mine[0])
            if depth > 3 * (own_count + 2):
                out_ref[head, 3 * (own_count + 2) :, :] = jnp.zeros(
                    (depth - 3 * (own_count + 2), BLOCK), F32
                )

    kv_specs = []
    for key_rows, _ in kvs:
        kv_specs += [pl.BlockSpec((key_rows.shape[0], wide), lambda h, band_ref: (0, h))] * 2
    stat_spec = pl.BlockSpec((per, depth, BLOCK), lambda h, band_ref: (h, 0, 0))
    frames = sum(kv[0].shape[0] for kv in kvs)
    flat = [array for kv in kvs for array in kv]
    extra = [] if earlier is None else [earlier]
    return call(
        body,
        (heads // per,),
        1,
        token_specs(own_count, wide, heads // per) + kv_specs + [stat_spec] * len(extra),
        stat_spec,
        jax.ShapeDtypeStruct((heads, depth, BLOCK), F32),
        8 * frames * 2 * BLOCK * columns,
        4 * frames * columns + 8 * queries.size,
        name="row_stats",
    )(band, below, queries, above, below, grads, above, *flat, *extra)


def gradients(band, tiles, kv, queries, grads, below, above, stats, from_below, from_above, scale):
    own_count = queries.shape[0] // BLOCK
    columns = queries.shape[1]
    heads = columns // DH
    per = min(2, heads)
    wide = per * DH
    frames = kv[0].shape[0]
    touched = tiles.touched
    own_touched = [t for t in touched if 0 <= t < own_count]
    halo_touched = [t for t in touched if t not in own_touched]

    def body(band_ref, *refs):
        tokens = refs[:6]
        key_ref, value_ref = refs[6:8]
        stat_ref, lower_ref, upper_ref = refs[8:11]
        key_out, value_out, own_out = refs[11:14]
        halo_outs = refs[14:]
        for head in range(per):
            lanes = slice(head * DH, (head + 1) * DH)
            rows = {}
            for t in touched:
                parts = [read_stats(stat_ref, head, 3 * (t + 1))]
                if t <= 0:
                    parts.append(read_stats(lower_ref, head, 3 * (own_count + t + 1)))
                if t >= own_count - 1:
                    parts.append(read_stats(upper_ref, head, 3 * (t - own_count + 1)))
                top, total, weighted = fold(parts)
                inverse = 1.0 / total
                rows[t] = (top, inverse, weighted * inverse)
            key_sum = [None] * (tiles.last - tiles.first)
            value_sum = [None] * (tiles.last - tiles.first)
            query_sum = {}
            for group, first, last, keys, query_rows, grad_rows, scores, slopes in head_tiles(
                band_ref, tiles, own_count, key_ref, value_ref, tokens[:3], tokens[3:], lanes, scale
            ):
                low, slope_low = [], []
                for f in range(first, last):
                    low_row, slope_row = [], []
                    for position, t in enumerate(group):
                        top, inverse, delta = rows[t]
                        p = jnp.exp(piece(scores, f - first, position) - top) * inverse
                        d = p * (piece(slopes, f - first, position) - delta) * scale
                        allowed = tile_allowed(band_ref, t, f, own_count)
                        if allowed is not None:
                            p = jnp.where(allowed, p, 0.0)
                            d = jnp.where(allowed, d, 0.0)
                        low_row.append(p.astype(BF16))
                        slope_row.append(d.astype(BF16))
                    low.append(jnp.concatenate(low_row, axis=1))
                    slope_low.append(jnp.concatenate(slope_row, axis=1))
                low = jnp.concatenate(low, axis=0)
                slope_low = jnp.concatenate(slope_low, axis=0)
                key_part = jnp.dot(slope_low, query_rows, preferred_element_type=F32)
                value_part = jnp.dot(low, grad_rows, preferred_element_type=F32)
                query_part = lax.dot_general(slope_low, keys, TN, preferred_element_type=F32)
                for f in range(first, last):
                    at, cut = f - tiles.first, slice((f - first) * BLOCK, (f - first + 1) * BLOCK)
                    key_sum[at] = (
                        key_part[cut] if key_sum[at] is None else key_sum[at] + key_part[cut]
                    )
                    value_sum[at] = (
                        value_part[cut] if value_sum[at] is None else value_sum[at] + value_part[cut]
                    )
                for position, t in enumerate(group):
                    query_sum[t] = query_part[position * BLOCK : (position + 1) * BLOCK]
            for at in range(tiles.last - tiles.first):
                cut = slice(at * BLOCK, (at + 1) * BLOCK)
                key_out[cut, lanes] = key_sum[at].astype(BF16)
                value_out[cut, lanes] = value_sum[at].astype(BF16)
            for at, t in enumerate(own_touched):
                own_out[at * BLOCK : (at + 1) * BLOCK, lanes] = query_sum[t]
            for out_ref, t in zip(halo_outs, halo_touched):
                out_ref[:, lanes] = query_sum[t]

    depth = stats.shape[1]
    stat_spec = pl.BlockSpec((per, depth, BLOCK), lambda h, band_ref: (h, 0, 0))
    kv_spec = pl.BlockSpec((frames, wide), lambda h, band_ref: (0, h))
    own_rows = len(own_touched) * BLOCK
    own_spec = pl.BlockSpec((own_rows, wide), lambda h, band_ref: (0, h))
    halo_spec = pl.BlockSpec((BLOCK, wide), lambda h, band_ref: (0, h))
    out = call(
        body,
        (heads // per,),
        1,
        token_specs(own_count, wide, heads // per) + [kv_spec] * 2 + [stat_spec] * 3,
        [kv_spec, kv_spec, own_spec] + [halo_spec] * len(halo_touched),
        [jax.ShapeDtypeStruct((frames, columns), BF16)] * 2
        + [jax.ShapeDtypeStruct((own_rows, columns), F32)]
        + [jax.ShapeDtypeStruct((BLOCK, columns), F32)] * len(halo_touched),
        20 * frames * 2 * BLOCK * columns,
        8 * frames * columns + 8 * queries.size + 4 * own_rows * columns,
        name="gradients",
    )(band, below, queries, above, below, grads, above, *kv, stats, from_below, from_above)
    return out[:2], (own_touched, out[2]), dict(zip(halo_touched, out[3:]))


def output_terms(index, slot, pieces, key_weight, value_weight, name):
    rows = sum(kg.shape[0] for kg, _ in pieces)
    columns = key_weight.shape[1]
    features = key_weight.shape[0] // lax.axis_size("tensor")
    tall = min(256, features)
    steps = features // tall
    count = len(pieces)

    def body(index_ref, *refs):
        key_ref, value_ref = refs[2 * count : 2 * count + 2]
        out_ref = refs[-1]
        at = 0
        for i in range(count):
            term = lax.dot_general(refs[2 * i][...], key_ref[...], NT, preferred_element_type=F32)
            term = term + lax.dot_general(
                refs[2 * i + 1][...], value_ref[...], NT, preferred_element_type=F32
            )
            size = term.shape[0]
            out_ref[at : at + size, :] = term.astype(BF16)
            at += size

    specs = []
    for kg, _ in pieces:
        specs += [pl.BlockSpec(kg.shape, lambda j, index_ref: (0, 0))] * 2
    weight_spec = pl.BlockSpec((tall, columns), lambda j, index_ref: (index_ref[slot] * steps + j, 0))
    return call(
        body,
        (steps,),
        1,
        specs + [weight_spec] * 2,
        pl.BlockSpec((rows, tall), lambda j, index_ref: (0, j)),
        jax.ShapeDtypeStruct((rows, features), BF16),
        4 * rows * columns * features,
        4 * rows * columns + 4 * columns * features + 2 * rows * features,
        name=name,
    )(index, *[a for pair in pieces for a in pair], key_weight, value_weight)


def add_rows(total, arrived, first):
    rows, features = arrived[0].shape
    tall = BLOCK
    count = len(arrived)

    def body(total_ref, *refs):
        value = total_ref[...].astype(F32)
        for ref in refs[:count]:
            value = value + ref[...].astype(F32)
        refs[count][...] = value.astype(BF16)

    here = pl.BlockSpec((tall, features), lambda i: (i + first // tall, 0))
    return call(
        body,
        (rows // tall,),
        0,
        [here] + [pl.BlockSpec((tall, features), lambda i: (i, 0))] * count,
        here,
        jax.ShapeDtypeStruct(total.shape, total.dtype),
        rows * features * count,
        2 * rows * features * (count + 2),
        aliases={0: 0},
        name="add_rows",
    )(total, *arrived)


def shifted(value, steps):
    count = lax.axis_size(ROWS)
    first, last = (max(0, -steps), min(count, count - steps))
    return lax.ppermute(value, ROWS, [(source, source + steps) for source in range(first, last)])


def on_device(encoder_states, key_weight, value_weight, queries, out_grad, band_blocks):
    frames = encoder_states.shape[0]
    tokens = queries.shape[0]
    own_count = tokens // BLOCK
    frame_blocks = frames // BLOCK
    scale = DH ** (-0.5)
    group = lax.axis_size("tensor")
    me = lax.axis_index("tensor")
    place, places = lax.axis_index(ROWS), lax.axis_size(ROWS)
    edge = HALO_BLK
    cuts = [(0, edge), (frame_blocks - edge, frame_blocks), (edge, frame_blocks - edge)]
    row_cuts = [(first * BLOCK, last * BLOCK) for first, last in cuts]
    turns = [[(i, (i + k) % group) for i in range(group)] for k in range(1, group)]
    sources = jnp.stack([lax.rem(me - k + group, group) for k in range(group)]).astype(jnp.int32)
    targets = jnp.stack([lax.rem(me + k, group) for k in range(group)]).astype(jnp.int32)

    arrived = []
    for first, last in row_cuts:
        rows = encoder_states[first:last]
        arrived.append([lax.ppermute(rows, "tensor", turn) for turn in turns])

    both = jnp.concatenate([queries, out_grad], axis=1)
    below = shifted(both[tokens - BLOCK :], 1)
    above = shifted(both[:BLOCK], -1)
    band_below = shifted(band_blocks[own_count - 1 :], 1)
    band_above = shifted(band_blocks[:1], -1)
    base = place * frame_blocks
    nowhere = jnp.array([[1, 0]], jnp.int32)
    band = jnp.concatenate(
        [
            jnp.where(place > 0, band_below - base, nowhere),
            band_blocks - base,
            jnp.where(place < places - 1, band_above - base, nowhere),
        ],
        axis=0,
    ).reshape(-1)

    partial = project_own(sources, encoder_states, key_weight, value_weight, row_cuts)
    kvs = [
        project_rest(sources, part, pieces, key_weight, value_weight)
        for part, pieces in zip(partial, arrived)
    ]

    tiles = [Tiles(own_count, first, last, i < 2) for i, (first, last) in enumerate(cuts)]
    shared = (queries, out_grad, below, above)
    edge_stats = row_stats(band, tiles[:2], kvs[:2], *shared, None, scale)
    stats = row_stats(band, tiles[2:], kvs[2:], *shared, edge_stats, scale)
    from_below = shifted(stats, 1)
    from_above = shifted(stats, -1)

    out = [None] * 3
    sent = [None] * 3
    for i in (2, 0, 1):
        out[i] = gradients(
            band, tiles[i], kvs[i], *shared, stats, from_below, from_above, scale
        )
        terms = [
            output_terms(targets, k, [out[i][0]], key_weight, value_weight, "terms_away")
            for k in range(1, group)
        ]
        sent[i] = [lax.ppermute(term, "tensor", turn) for term, turn in zip(terms, turns)]

    back_up = shifted(out[1][2][own_count], 1)
    back_down = shifted(out[0][2][-1], -1)
    blocks = [[] for _ in range(own_count)]
    for _, (touched, part), _ in out:
        for at, t in enumerate(touched):
            blocks[t].append(part[at * BLOCK : (at + 1) * BLOCK])
    blocks[0].append(back_up)
    blocks[-1].append(back_down)
    query_grad = jnp.concatenate([sum(parts).astype(BF16) for parts in blocks], axis=0)

    encoder_grad = output_terms(
        targets, 0, [out[0][0], out[2][0], out[1][0]], key_weight, value_weight, "terms_own"
    )
    for i in (2, 0, 1):
        encoder_grad = add_rows(encoder_grad, sent[i], row_cuts[i][0])
    return (query_grad, encoder_grad)


def solution(mesh):
    return jax.shard_map(
        on_device,
        mesh=mesh,
        in_specs=(
            P(ROWS, "tensor"),
            P(None, "tensor"),
            P(None, "tensor"),
            P(ROWS, "tensor"),
            P(ROWS, "tensor"),
            P(ROWS, None),
        ),
        out_specs=(P(ROWS, "tensor"), P(ROWS, "tensor")),
        check_vma=False,
    )
```

time: 592 us -> 258 us (0.44)
  waiting for transfers between devices: 294 us -> 31.4 us
  Pallas kernels: 0 us -> 178 us
  matrix products: 150 us -> 0 us
  other arithmetic: 43.5 us -> 5.41 us
  local copies, waits for them, and re-layouts: 33.6 us -> 10 us
  starting transfers between devices: 48.6 us -> 27.9 us
  between operations: 14.4 us -> 0.84 us
    pallas_call x0 -> x16, Pallas kernels: none -> 178 us  [the longest x4 57.3 us: output_terms(): call(body, (steps,), 1, specs + [weight_spec] * 2, pl.BlockSpec((rows, ta...]
    dot_general x10 -> x0, matrix products: 150 us -> none  [the longest x1 21.6 us: on_device(): lax.dot_general(value_grad, value_weight, contract, preferred_element_typ...]
    reduce_scatter x1 -> x0, waiting for transfers between devices: 109 us -> none  [on_device(): lax.psum_scatter(group_term.astype(jnp.bfloat16), 'tensor', scatter_dimen...]
    all_gather x1 -> x0, waiting for transfers between devices: 84.7 us -> none  [on_device(): pieces_in = lax.all_gather(encoder_states, 'tensor', axis=1, tiled=True)]
    ppermute x4 -> x14, waiting for transfers between devices: 99.9 us -> 31.4 us  [the longest x3 17.3 us: on_device(): arrived.append([lax.ppermute(rows, 'tensor', turn) for turn in turns])]
    concatenate x3 -> x2, other arithmetic: 24.6 us -> 1.05 us  [the longest x1 1.04 us: on_device(): jnp.concatenate([sum(parts).astype(BF16) for parts in blocks], axis=0)]
    ppermute x4 -> x14, starting transfers between devices: 48.5 us -> 27.9 us  [the longest x8 20.8 us: shifted(): lax.ppermute(value, ROWS, [(source, source + steps) for source in range(f...]
    reshape x3 -> x1, local copies, waits for them, and re-layouts: 18 us -> 0.66 us  [on_device(): band = jnp.concatenate([jnp.where(place > 0, band_below - base, nowhere),...]
  transfers between devices with their start and end apart: 6 -> 14, of which waited for: 4 -> 4; matrix products, arithmetic and copies ran while one was open for 2% -> 4% of each run, Pallas kernels for 0% -> 57%
where the time goes in v1:
time: 258 us; the launch traced here: 253 us
  Pallas kernels  178 us (69%)
  waiting for transfers between devices  31.4 us (12%)
  starting transfers between devices  27.9 us (11%)
  local copies, waits for them, and re-layouts  10 us (4%)
  other arithmetic  5.41 us (2%)
    pallas_call x4, Pallas kernels, output_terms(): call(body, (steps,), 1, specs + [weight_spec] * 2, pl.BlockSpec((rows, ta...  57.3 us
    pallas_call x3, Pallas kernels, project_rest(): call(body, (columns // wide,), 1, [tile, tile] + [piece_spec] * count + w...  40 us
    pallas_call x3, Pallas kernels, gradients(): call(body, (heads // per,), 1, token_specs(own_count, wide, heads // per)...  34.7 us
    ppermute x8, starting transfers between devices, shifted(): lax.ppermute(value, ROWS, [(source, source + steps) for source in range(f...  20.8 us
    pallas_call x1, Pallas kernels, project_own(): call(body, (columns // wide,), 1, [pl.BlockSpec((rows, depth), lambda j,...  19.5 us
    pallas_call x2, Pallas kernels, row_stats(): call(body, (heads // per,), 1, token_specs(own_count, wide, heads // per)...  18.9 us
    ppermute x3, waiting for transfers between devices, on_device(): arrived.append([lax.ppermute(rows, 'tensor', turn) for turn in turns])  17.3 us
    ppermute x3, waiting for transfers between devices, on_device(): lax.ppermute(term, 'tensor', turn)  12.6 us
  transfers between devices with their start and end apart: 14, of which 4 were waited for; matrix products, arithmetic and copies ran while one was open for 4% of the time, Pallas kernels for 57%

profile of v1, /device:TPU:0, one launch (start us, length us, event | category | flops | bytes accessed | tf_op | source)
XLA Modules:
  0.0 253.5 jit_solution(10532037921563106103)
XLA Ops:
  0.6 0.0 copy-start.2
  0.6 0.8 fusion.2
  1.4 2.4 collective-permute-start
  3.8 1.3 collective-permute-start.1
  5.1 1.3 constant_dynamic-update-slice_fusion.1
  6.4 0.0 copy-done.2
  6.4 0.1 constant_dynamic-update-slice_fusion
  6.5 0.0 copy-start.3
  6.5 1.5 fusion.1
  8.0 5.3 %collective-permute-start.2 = (bf16[128,4096]{1,0:T(8,128)(2,1)}, bf16[128,4096]{1,0:T(8,128)(2,1)S(1)}, u32[]{:S(2)}, u32[]{:S(2)}) collective-permute-start(bf16[128,4096]{1,0:T(8,128)(2,1)} %get-tuple-element.54), channel_id=1, source_target_pairs={{0,1},{1,4},{4,5},{5,8},{8,9},{9,12},{12,13},{13,16},{16,17},{17,2... | collective-permute-start | bytes 3145736 | tf_op jit(solution)/shard_map/ppermute | solution.py:433
  13.3 1.8 fusion
  15.1 1.5 collective-permute-start.6
  16.6 0.5 collective-permute-start.5
  17.2 0.6 pad_add_fusion.1.index_ref
  17.7 19.5 %project_own.1 = (f32[256,2048]{1,0:T(8,128)}, f32[256,2048]{1,0:T(8,128)}, f32[256,2048]{1,0:T(8,128)}, f32[256,2048]{1,0:T(8,128)}, f32[256,2048]{1,0:T(8,128)}, /*index=5*/f32[256,2048]{1,0:T(8,128)}) custom-call(s32[2]{0:T(128)} %pad_add_fusion.1.index_ref, bf16[768,2048]{1,0:T(8,128)(2,1)} %states_ref.1, bf16[4096,2048]{1,0:T(8,128)(2,1)} %refs_2_.5, ...), custom_call_target="tpu_custom_call" | custom-call | flops 12884901888 | bytes 32505856 | tf_op jit(solution)/shard_map/project_own/pallas_call | solution.py:52
  37.2 0.0 collective-permute-done
  37.2 1.3 collective-permute-start.3
  38.5 0.0 collective-permute-done.1
  38.5 1.6 collective-permute-start.4
  40.1 0.7 reshape.7.band_ref
  40.8 0.0 collective-permute-done.6.refs_2_
  40.8 13.3 %project_rest.5 = (bf16[256,2048]{1,0:T(8,128)(2,1)}, bf16[256,2048]{1,0:T(8,128)(2,1)}) custom-call(s32[2]{0:T(128)} %pad_add_fusion.1.index_ref, f32[256,2048]{1,0:T(8,128)} %get-tuple-element.33.refs_0_, f32[256,2048]{1,0:T(8,128)} %get-tuple-element.34.refs_1_, bf16[256,2048]{1,0:T(8,128)(2,1)} %collective-permute-done.6.refs_2_, ...), custom_call_target="tpu_custom_call" | custom-call | flops 4294967296 | bytes 24117248 | tf_op jit(solution)/shard_map/project_rest/pallas_call | solution.py:89
  54.1 9.1 %collective-permute-done.5.refs_2_ = bf16[256,2048]{1,0:T(8,128)(2,1)S(1)} collective-permute-done((bf16[256,2048]{1,0:T(8,128)(2,1)}, bf16[256,2048]{1,0:T(8,128)(2,1)S(1)}, u32[]{:S(2)}, u32[]{:S(2)}) %collective-permute-start.5) | collective-permute-done | bytes 1048608 | tf_op jit(solution)/shard_map/ppermute | solution.py:455
  63.2 1.0 copy-done.5
  64.2 13.4 %project_rest.4 = (bf16[256,2048]{1,0:T(8,128)(2,1)}, bf16[256,2048]{1,0:T(8,128)(2,1)}) custom-call(s32[2]{0:T(128)} %pad_add_fusion.1.index_ref, f32[256,2048]{1,0:T(8,128)} %get-tuple-element.29.refs_0_, f32[256,2048]{1,0:T(8,128)} %get-tuple-element.30.refs_1_, bf16[256,2048]{1,0:T(8,128)(2,1)} %copy-done.5, bf16[4096,2048]{1,0:T(8,128)(2,1)} %refs_2_.5, ...), custom_call_target="tpu_custom_call" | custom-call | flops 4294967296 | bytes 24117248 | tf_op jit(solution)/shard_map/project_rest/pallas_call | solution.py:89
  77.5 8.2 %collective-permute-done.4.refs_2_ = bf16[256,2048]{1,0:T(8,128)(2,1)} collective-permute-done((bf16[256,2048]{1,0:T(8,128)(2,1)}, bf16[256,2048]{1,0:T(8,128)(2,1)}, u32[]{:S(2)}, u32[]{:S(2)}) %collective-permute-start.4) | collective-permute-done | bytes 1048608 | tf_op jit(solution)/shard_map/ppermute | solution.py:455
  85.7 13.3 %project_rest.3 = (bf16[256,2048]{1,0:T(8,128)(2,1)}, bf16[256,2048]{1,0:T(8,128)(2,1)}) custom-call(s32[2]{0:T(128)} %pad_add_fusion.1.index_ref, f32[256,2048]{1,0:T(8,128)} %get-tuple-element.25.refs_0_, f32[256,2048]{1,0:T(8,128)} %get-tuple-element.26.refs_1_, bf16[256,2048]{1,0:T(8,128)(2,1)} %collective-permute-done.4.refs_2_, ...), custom_call_target="tpu_custom_call" | custom-call | flops 4294967296 | bytes 24117248 | tf_op jit(solution)/shard_map/project_rest/pallas_call | solution.py:89
  99.1 0.0 collective-permute-done.2.refs_0_.refs_3_
  99.1 0.0 copy-start
  99.1 0.0 collective-permute-done.3.refs_2_.refs_5_
  99.1 0.0 copy-start.1
  99.1 0.9 copy-done
  100.0 0.3 copy-done.1
  100.4 10.5 %row_stats.2.refs_8_ = f32[16,16,128]{2,1,0:T(8,128)} custom-call(s32[8]{0:T(128)} %reshape.7.band_ref, bf16[128,4096]{1,0:T(8,128)(2,1)} %copy-done, bf16[256,2048]{1,0:T(8,128)(2,1)} %refs_1_.9, bf16[128,4096]{1,0:T(8,128)(2,1)} %copy-done.1, bf16[128,4096]{1,0:T(8,128)(2,1)} %copy-done, bf16[256,2048]{1,0:T(8,128)(2,1)} %refs_4_.15, ...), custom_call_target="tpu_custom_call" | custom-call | flops 2147483648 | bytes 8388608 | tf_op jit(solution)/shard_map/row_stats/pallas_call | solution.py:257
  110.9 8.4 %row_stats.3.refs_8_ = f32[16,16,128]{2,1,0:T(8,128)} custom-call(s32[8]{0:T(128)} %reshape.7.band_ref, bf16[128,4096]{1,0:T(8,128)(2,1)} %copy-done, bf16[256,2048]{1,0:T(8,128)(2,1)} %refs_1_.9, bf16[128,4096]{1,0:T(8,128)(2,1)} %copy-done.1, bf16[128,4096]{1,0:T(8,128)(2,1)} %copy-done, bf16[256,2048]{1,0:T(8,128)(2,1)} %refs_4_.15, ...), custom_call_target="tpu_custom_call" | custom-call | flops 1073741824 | bytes 6291456 | tf_op jit(solution)/shard_map/row_stats/pallas_call | solution.py:257
  119.3 2.4 collective-permute-start.7
  121.7 1.3 collective-permute-start.8
  123.0 0.6 pad_add_fusion.2.index_ref
  123.7 0.0 collective-permute-done.7.refs_9_
  123.7 1.5 collective-permute-done.8.refs_10_
  125.2 0.7 copy-done.10
  125.8 12.1 %gradients.4 = (bf16[256,2048]{1,0:T(8,128)(2,1)}, bf16[256,2048]{1,0:T(8,128)(2,1)}, f32[256,2048]{1,0:T(8,128)}, f32[128,2048]{1,0:T(8,128)}) custom-call(s32[8]{0:T(128)} %reshape.7.band_ref, bf16[128,4096]{1,0:T(8,128)(2,1)} %copy-done, bf16[256,2048]{1,0:T(8,128)(2,1)} %refs_1_.9, bf16[128,4096]{1,0:T(8,128)(2,1)} %copy-done.1, ...), custom_call_target="tpu_custom_call" | custom-call | flops 2684354560 | bytes 10485760 | tf_op jit(solution)/shard_map/gradients/pallas_call | solution.py:350
  137.9 5.3 %collective-permute-start.9 = (f32[128,2048]{1,0:T(8,128)}, f32[128,2048]{1,0:T(8,128)S(1)}, u32[]{:S(2)}, u32[]{:S(2)}) collective-permute-start(f32[128,2048]{1,0:T(8,128)} %get-tuple-element.40), channel_id=1, source_target_pairs={{0,1},{1,4},{4,5},{5,8},{8,9},{9,12},{12,13},{13,16},{16,17},{17,2... | collective-permute-start | bytes 3145736 | tf_op jit(solution)/shard_map/ppermute | solution.py:433
  143.3 12.0 %gradients.3 = (bf16[256,2048]{1,0:T(8,128)(2,1)}, bf16[256,2048]{1,0:T(8,128)(2,1)}, f32[256,2048]{1,0:T(8,128)}, f32[128,2048]{1,0:T(8,128)}) custom-call(s32[8]{0:T(128)} %reshape.7.band_ref, bf16[128,4096]{1,0:T(8,128)(2,1)} %copy-done, bf16[256,2048]{1,0:T(8,128)(2,1)} %refs_1_.9, bf16[128,4096]{1,0:T(8,128)(2,1)} %copy-done.1, ...), custom_call_target="tpu_custom_call" | custom-call | flops 2684354560 | bytes 10485760 | tf_op jit(solution)/shard_map/gradients/pallas_call | solution.py:350
  155.3 1.5 collective-permute-start.10
  156.8 10.6 %gradients.5 = (bf16[256,2048]{1,0:T(8,128)(2,1)}, bf16[256,2048]{1,0:T(8,128)(2,1)}, f32[256,2048]{1,0:T(8,128)}) custom-call(s32[8]{0:T(128)} %reshape.7.band_ref, bf16[128,4096]{1,0:T(8,128)(2,1)} %copy-done, bf16[256,2048]{1,0:T(8,128)(2,1)} %refs_1_.9, bf16[128,4096]{1,0:T(8,128)(2,1)} %copy-done.1, bf16[128,4096]{1,0:T(8,128)(2,1)} %copy-done, ...), custom_call_target="tpu_custom_call" | custom-call | flops 2684354560 | bytes 10485760 | tf_op jit(solution)/shard_map/gradients/pallas_call | solution.py:350
  167.4 12.5 %terms_away.3 = bf16[256,2048]{1,0:T(8,128)(2,1)} custom-call(s32[2]{0:T(128)} %pad_add_fusion.2.index_ref, bf16[256,2048]{1,0:T(8,128)(2,1)} %get-tuple-element.44.refs_2_.refs_0_, bf16[256,2048]{1,0:T(8,128)(2,1)} %get-tuple-element.45.refs_3_.refs_1_, bf16[4096,2048]{1,0:T(8,128)(2,1)} %refs_2_.5, bf16[4096,2048]{1,0:T(8,128)(2,1)} %refs_3_.11), custom_call_target="tpu_custom_call" | custom-call | flops 4294967296 | bytes 19922944 | tf_op jit(solution)/shard_map/terms_away/pallas_call | solution.py:391
  179.9 1.5 collective-permute-start.11
  181.4 12.6 %terms_away.4 = bf16[256,2048]{1,0:T(8,128)(2,1)} custom-call(s32[2]{0:T(128)} %pad_add_fusion.2.index_ref, bf16[256,2048]{1,0:T(8,128)(2,1)} %get-tuple-element.42.refs_0_, bf16[256,2048]{1,0:T(8,128)(2,1)} %get-tuple-element.43.refs_1_, bf16[4096,2048]{1,0:T(8,128)(2,1)} %refs_2_.5, bf16[4096,2048]{1,0:T(8,128)(2,1)} %refs_3_.11), custom_call_target="tpu_custom_call" | custom-call | flops 4294967296 | bytes 19922944 | tf_op jit(solution)/shard_map/terms_away/pallas_call | solution.py:391
  194.0 0.5 collective-permute-start.12
  194.5 12.5 %terms_away.5 = bf16[256,2048]{1,0:T(8,128)(2,1)} custom-call(s32[2]{0:T(128)} %pad_add_fusion.2.index_ref, bf16[256,2048]{1,0:T(8,128)(2,1)} %get-tuple-element.46.refs_4_.refs_0_, bf16[256,2048]{1,0:T(8,128)(2,1)} %get-tuple-element.47.refs_5_.refs_1_, bf16[4096,2048]{1,0:T(8,128)(2,1)} %refs_2_.5, bf16[4096,2048]{1,0:T(8,128)(2,1)} %refs_3_.11), custom_call_target="tpu_custom_call" | custom-call | flops 4294967296 | bytes 19922944 | tf_op jit(solution)/shard_map/terms_away/pallas_call | solution.py:391
  207.0 1.5 collective-permute-start.13
  208.5 19.7 %terms_own.1.total_ref = bf16[768,2048]{1,0:T(8,128)(2,1)} custom-call(s32[2]{0:T(128)} %pad_add_fusion.2.index_ref, bf16[256,2048]{1,0:T(8,128)(2,1)} %get-tuple-element.42.refs_0_, bf16[256,2048]{1,0:T(8,128)(2,1)} %get-tuple-element.43.refs_1_, bf16[256,2048]{1,0:T(8,128)(2,1)} %get-tuple-element.44.refs_2_.refs_0_, ...), custom_call_target="tpu_custom_call" | custom-call | flops 12884901888 | bytes 26214400 | tf_op jit(solution)/shard_map/terms_own/pallas_call | solution.py:391
  228.2 0.0 collective-permute-done.11.refs_0_
  228.2 1.0 copy-done.6
  229.2 2.4 add_rows.3.total_ref
  231.6 0.0 collective-permute-done.12.refs_0_
  231.6 2.6 %add_rows.4.total_ref = bf16[768,2048]{1,0:T(8,128)(2,1)} custom-call(bf16[768,2048]{1,0:T(8,128)(2,1)} %add_rows.3.total_ref, bf16[256,2048]{1,0:T(8,128)(2,1)} %collective-permute-done.12.refs_0_), custom_call_target="tpu_custom_call", output_to_operand_aliasing={{}: (0, {})} | custom-call | flops 524288 | bytes 3145728 | tf_op jit(solution)/shard_map/add_rows/pallas_call | solution.py:416
  234.2 0.0 collective-permute-done.9
  234.2 0.0 collective-permute-done.10
  234.2 3.1 %add_convert_fusion.1 = (bf16[128,2048]{1,0:T(8,128)(2,1)S(1)}, bf16[128,2048]{1,0:T(8,128)(2,1)S(1)}) fusion(f32[128,2048]{1,0:T(8,128)S(1)} %collective-permute-done.9, f32[256,2048]{1,0:T(8,128)} %get-tuple-element.39, f32[256,2048]{1,0:T(8,128)S(1)} %copy-done.4, f32[256,2048]{1,0:T(8,128)} %get-tuple-element.37, f32[128,2048]{1,0:T(8,128)} %collective-permute-done.10), kind=kLoop, calls=%fused_computation.2 | loop fusion | flops 2097152 | bytes 9437184 | tf_op jit(solution)/shard_map/convert_element_type | solution.py:506
  237.4 1.0 pad_maximum_fusion
  238.4 12.6 %collective-permute-done.13.refs_0_ = bf16[256,2048]{1,0:T(8,128)(2,1)} collective-permute-done((bf16[256,2048]{1,0:T(8,128)(2,1)}, bf16[256,2048]{1,0:T(8,128)(2,1)}, u32[]{:S(2)}, u32[]{:S(2)}) %collective-permute-start.13) | collective-permute-done | bytes 1048608 | tf_op jit(solution)/shard_map/ppermute | solution.py:496
  251.0 2.4 add_rows.5
  (15 shorter events, 0.0 us)
Async XLA Ops:
  0.6 5.8 %copy-start.2 = (bf16[256,2048]{1,0:T(8,128)(2,1)S(1)}, bf16[256,2048]{1,0:T(8,128)(2,1)}, u32[]{:S(2)}) copy-start(bf16[256,2048]{1,0:T(8,128)(2,1)} %refs_4_.15) | copy-start | bytes 3145732
  1.4 35.8 %collective-permute-start = (s32[1,2]{1,0:T(1,128)S(1)}, s32[1,2]{1,0:T(1,128)S(1)}, u32[]{:S(2)}, u32[]{:S(2)}) collective-permute-start(s32[1,2]{1,0:T(1,128)S(1)} %get-tuple-element.55), channel_id=1, source_target_pairs={{0,1},{1,4},{4,5},{5,8},{8,9},{9,12},{12,13},{13,16},{16,17},{17,2... | collective-permute-start | bytes 32 | tf_op jit(solution)/shard_map/ppermute | solution.py:433
  3.8 34.7 %collective-permute-start.1 = (s32[1,2]{1,0:T(1,128)S(1)}, s32[1,2]{1,0:T(1,128)S(1)}, u32[]{:S(2)}, u32[]{:S(2)}) collective-permute-start(s32[1,2]{1,0:T(1,128)S(1)} %get-tuple-element.56), channel_id=1, source_target_pairs={{1,0},{4,1},{5,4},{8,5},{9,8},{12,9},{13,12},{16,13},{17,16},{20,1... | collective-permute-start | bytes 32 | tf_op jit(solution)/shard_map/ppermute | solution.py:433
  6.5 6.8 %copy-start.3 = (bf16[768,2048]{1,0:T(8,128)(2,1)S(1)}, bf16[768,2048]{1,0:T(8,128)(2,1)}, u32[]{:S(2)}) copy-start(bf16[768,2048]{1,0:T(8,128)(2,1)} %states_ref.1) | copy-start | bytes 9437188
  8.0 91.1 %collective-permute-start.2 = (bf16[128,4096]{1,0:T(8,128)(2,1)}, bf16[128,4096]{1,0:T(8,128)(2,1)S(1)}, u32[]{:S(2)}, u32[]{:S(2)}) collective-permute-start(bf16[128,4096]{1,0:T(8,128)(2,1)} %get-tuple-element.54), channel_id=1, source_target_pairs={{0,1},{1,4},{4,5},{5,8},{8,9},{9,12},{12,13},{13,16},{16,17},{17,2... | collective-permute-start | bytes 3145736 | tf_op jit(solution)/shard_map/ppermute | solution.py:433
  15.1 25.6 %collective-permute-start.6 = (bf16[256,2048]{1,0:T(8,128)(2,1)}, bf16[256,2048]{1,0:T(8,128)(2,1)}, u32[]{:S(2)}, u32[]{:S(2)}) collective-permute-start(bf16[256,2048]{1,0:T(8,128)(2,1)} %get-tuple-element.50), channel_id=1, source_target_pairs={{0,2},{2,0},{1,3},{3,1},{4,6},{6,4},{5,7},{7,5},{8,10},{10,8},{9,1... | collective-permute-start | bytes 3145736 | tf_op jit(solution)/shard_map/ppermute | solution.py:455
  16.6 46.5 %collective-permute-start.5 = (bf16[256,2048]{1,0:T(8,128)(2,1)}, bf16[256,2048]{1,0:T(8,128)(2,1)S(1)}, u32[]{:S(2)}, u32[]{:S(2)}) collective-permute-start(bf16[256,2048]{1,0:T(8,128)(2,1)} %get-tuple-element.52), channel_id=1, source_target_pairs={{0,2},{2,0},{1,3},{3,1},{4,6},{6,4},{5,7},{7,5},{8,10},{10,8},{9,1... | collective-permute-start | bytes 3145736 | tf_op jit(solution)/shard_map/ppermute | solution.py:455
  17.7 19.5 %copy-start.7 = (s32[2,2]{1,0:T(2,128)S(1)}, s32[2,2]{1,0:T(2,128)}, u32[]{:S(2)}) copy-start(s32[2,2]{1,0:T(2,128)} %param.12) | copy-start | bytes 52
  17.7 22.4 %copy-start.8 = (s32[1,2]{1,0:T(1,128)S(1)}, s32[1,2]{1,0:T(1,128)}, u32[]{:S(2)}) copy-start(s32[1,2]{1,0:T(1,128)} %constant.34.clone) | copy-start | bytes 28
  37.2 61.9 %collective-permute-start.3 = (bf16[128,4096]{1,0:T(8,128)(2,1)}, bf16[128,4096]{1,0:T(8,128)(2,1)S(1)}, u32[]{:S(2)}, u32[]{:S(2)}) collective-permute-start(bf16[128,4096]{1,0:T(8,128)(2,1)} %get-tuple-element.53), channel_id=1, source_target_pairs={{1,0},{4,1},{5,4},{8,5},{9,8},{12,9},{13,12},{16,13},{17,16},{20,1... | collective-permute-start | bytes 3145736 | tf_op jit(solution)/shard_map/ppermute | solution.py:433
  38.5 47.2 %collective-permute-start.4 = (bf16[256,2048]{1,0:T(8,128)(2,1)}, bf16[256,2048]{1,0:T(8,128)(2,1)}, u32[]{:S(2)}, u32[]{:S(2)}) collective-permute-start(bf16[256,2048]{1,0:T(8,128)(2,1)} %get-tuple-element.51), channel_id=1, source_target_pairs={{0,2},{2,0},{1,3},{3,1},{4,6},{6,4},{5,7},{7,5},{8,10},{10,8},{9,1... | collective-permute-start | bytes 3145736 | tf_op jit(solution)/shard_map/ppermute | solution.py:455
  63.2 1.0 copy-start.5
  99.1 1.0 copy-start
  99.1 1.3 copy-start.1
  119.3 4.4 %collective-permute-start.7 = (f32[16,16,128]{2,1,0:T(8,128)}, f32[16,16,128]{2,1,0:T(8,128)S(1)}, u32[]{:S(2)}, u32[]{:S(2)}) collective-permute-start(f32[16,16,128]{2,1,0:T(8,128)} %row_stats.3.refs_8_), channel_id=1, source_target_pairs={{0,1},{1,4},{4,5},{5,8},{8,9},{9,12},{12,13},{13,16},{16,17},{17,2... | collective-permute-start | bytes 393224 | tf_op jit(solution)/shard_map/ppermute | solution.py:433
  121.7 3.5 %collective-permute-start.8 = (f32[16,16,128]{2,1,0:T(8,128)}, f32[16,16,128]{2,1,0:T(8,128)S(1)}, u32[]{:S(2)}, u32[]{:S(2)}) collective-permute-start(f32[16,16,128]{2,1,0:T(8,128)} %row_stats.3.refs_8_), channel_id=1, source_target_pairs={{1,0},{4,1},{5,4},{8,5},{9,8},{12,9},{13,12},{16,13},{17,16},{20,1... | collective-permute-start | bytes 393224 | tf_op jit(solution)/shard_map/ppermute | solution.py:433
  123.7 1.5 copy-start.9
  125.2 0.7 copy-start.10
  137.9 96.3 %collective-permute-start.9 = (f32[128,2048]{1,0:T(8,128)}, f32[128,2048]{1,0:T(8,128)S(1)}, u32[]{:S(2)}, u32[]{:S(2)}) collective-permute-start(f32[128,2048]{1,0:T(8,128)} %get-tuple-element.40), channel_id=1, source_target_pairs={{0,1},{1,4},{4,5},{5,8},{8,9},{9,12},{12,13},{13,16},{16,17},{17,2... | collective-permute-start | bytes 3145736 | tf_op jit(solution)/shard_map/ppermute | solution.py:433
  155.3 79.0 %collective-permute-start.10 = (f32[128,2048]{1,0:T(8,128)}, f32[128,2048]{1,0:T(8,128)}, u32[]{:S(2)}, u32[]{:S(2)}) collective-permute-start(f32[128,2048]{1,0:T(8,128)} %get-tuple-element.41), channel_id=1, source_target_pairs={{1,0},{4,1},{5,4},{8,5},{9,8},{12,9},{13,12},{16,13},{17,16},{20,1... | collective-permute-start | bytes 3145736 | tf_op jit(solution)/shard_map/ppermute | solution.py:433
  179.9 48.3 %collective-permute-start.11 = (bf16[256,2048]{1,0:T(8,128)(2,1)}, bf16[256,2048]{1,0:T(8,128)(2,1)S(1)}, u32[]{:S(2)}, u32[]{:S(2)}) collective-permute-start(bf16[256,2048]{1,0:T(8,128)(2,1)} %terms_away.3), channel_id=1, source_target_pairs={{0,2},{2,0},{1,3},{3,1},{4,6},{6,4},{5,7},{7,5},{8,10},{10,8},{9,1... | collective-permute-start | bytes 3145736 | tf_op jit(solution)/shard_map/ppermute | solution.py:496
  194.0 37.7 %collective-permute-start.12 = (bf16[256,2048]{1,0:T(8,128)(2,1)}, bf16[256,2048]{1,0:T(8,128)(2,1)}, u32[]{:S(2)}, u32[]{:S(2)}) collective-permute-start(bf16[256,2048]{1,0:T(8,128)(2,1)} %terms_away.4), channel_id=1, source_target_pairs={{0,2},{2,0},{1,3},{3,1},{4,6},{6,4},{5,7},{7,5},{8,10},{10,8},{9,1... | collective-permute-start | bytes 3145736 | tf_op jit(solution)/shard_map/ppermute | solution.py:496
  207.0 44.0 %collective-permute-start.13 = (bf16[256,2048]{1,0:T(8,128)(2,1)}, bf16[256,2048]{1,0:T(8,128)(2,1)}, u32[]{:S(2)}, u32[]{:S(2)}) collective-permute-start(bf16[256,2048]{1,0:T(8,128)(2,1)} %terms_away.5), channel_id=1, source_target_pairs={{0,2},{2,0},{1,3},{3,1},{4,6},{6,4},{5,7},{7,5},{8,10},{10,8},{9,1... | collective-permute-start | bytes 3145736 | tf_op jit(solution)/shard_map/ppermute | solution.py:496
  228.2 1.0 copy-start.6
  231.6 2.6 %copy-start.4 = (f32[256,2048]{1,0:T(8,128)S(1)}, f32[256,2048]{1,0:T(8,128)}, u32[]{:S(2)}) copy-start(f32[256,2048]{1,0:T(8,128)} %get-tuple-element.38) | copy-start | bytes 6291460
